TPU v7x, 32 devices: a whole 2x2x4 slice. The times are simulated.
32 devices in a mesh: streams: 2 (over y), span: 4 (over z), head: 2 (over x), seq: 2 (over core).
Axes of the slice: x: 2, y: 2, z: 4, core: 2. Of those that a mesh axis runs over, the one named last changes fastest.
Arguments:
- query_rows: bfloat16 [4096, 1280], P(('streams', 'span', 'seq'), 'head'), parts along dimension 0, may hold values from -100 to 100
- key_rows: bfloat16 [4096, 1280], P(('streams', 'span', 'seq'), 'head'), parts along dimension 0, may hold values from -5 to 5
- value_rows: bfloat16 [4096, 1280], P(('streams', 'span', 'seq'), 'head'), parts along dimension 0, may hold values from -6 to 6
- out_weight: bfloat16 [1280, 5120], P('head', 'seq'), may hold values from -0.59765625 to 0.59765625
- gate_table: float32 [4, 5120], P(None, 'head'), may hold values from 0.5 to 2
- step_index: int32 [8], P('streams'), parts along dimension 0, may hold values from 0 to 3
- block_mask: int32 [8, 4], P('streams'), parts along dimension 0, may hold values from 0 to 1, as said below
Outputs:
- gated_update: bfloat16 [4096, 5120], P(('streams', 'span', 'seq'), 'head'), parts along dimension 0
There are 2 independent parts, one for each index of `streams`. A program takes and returns all parts, laid end to end along the dimension named above; an argument that names none is the same for every part. Nothing has to cross between parts.
Inputs may be any that keep to these rules, and one draw needn't show every extreme that they name: block_mask[c, c] = 1 and block_mask[c, e] = 0 for e > c; entries below the diagonal are 0 or 1.
All inputs are finite; a program needn't handle non-finite values.
Results may differ from a plain program's by a relative error of at most 0.017.
Values may be sent and summed in bfloat16 or wider, within the bound.
No kernel may reach another device: no remote copies, remote signals or barrier semaphores. Data moves between devices by JAX's collectives and lax.ppermute only.
A program may use at most 192 MiB of HBM per device.

v0:
```python
import math

import jax
import jax.numpy as jnp
from jax import lax
from jax.sharding import PartitionSpec as P

HD = 128


NEG_FLOOR = -1e30


def on_device(query_rows, key_rows, value_rows, out_weight, gate_table, step_index, block_mask):
    tok_rows = query_rows.shape[0]
    heads_here = query_rows.shape[1] // HD
    group_count = lax.axis_size("span")
    span_tok = tok_rows * lax.axis_size("seq")
    my_span = lax.axis_index("span")
    group_ids = jnp.arange(group_count, dtype=jnp.int32)
    mask_row = jnp.sum(jnp.where(group_ids[:, None] == my_span, block_mask, 0), axis=0)
    query_three = query_rows.reshape(tok_rows, heads_here, HD)
    score_scale = 1.0 / math.sqrt(HD)
    run_max = jnp.full((heads_here, tok_rows), NEG_FLOOR, jnp.float32)
    key_part = lax.all_gather(key_rows, ("span", "seq"), axis=0, tiled=True)
    value_part = lax.all_gather(value_rows, ("span", "seq"), axis=0, tiled=True)
    piece_rows = key_part.shape[0]
    key_group = jnp.arange(piece_rows, dtype=jnp.int32) // span_tok
    visible = (
        jnp.sum(jnp.where(key_group[:, None] == group_ids[None, :], mask_row[None, :], 0), axis=1)
        == 1
    )
    scores = (
        jnp.einsum(
            "thd,khd->htk",
            query_three,
            key_part.reshape(piece_rows, heads_here, HD),
            preferred_element_type=jnp.float32,
        )
        * score_scale
    )
    scores = jnp.where(visible[None, None, :], scores, NEG_FLOOR)
    new_max = jnp.maximum(run_max, jnp.max(scores, axis=2))
    probs = jnp.where(visible[None, None, :], jnp.exp(scores - new_max[:, :, None]), 0.0)
    run_total = jnp.sum(probs, axis=2)
    added = jnp.einsum(
        "htk,khd->htd",
        probs.astype(jnp.bfloat16),
        value_part.reshape(piece_rows, heads_here, HD),
        preferred_element_type=jnp.float32,
    )
    run_accum = added
    run_max, run_total, run_accum = (new_max, run_total, run_accum)
    summed = run_accum / run_total[:, :, None]
    attended = (
        jnp.transpose(summed, (1, 0, 2)).reshape(tok_rows, heads_here * HD).astype(jnp.bfloat16)
    )
    projected = jnp.dot(
        attended,
        lax.all_gather(out_weight, "seq", axis=1, tiled=True),
        preferred_element_type=jnp.float32,
    )
    shared = lax.psum_scatter(
        projected.astype(jnp.bfloat16), "head", scatter_dimension=1, tiled=True
    ).astype(jnp.float32)
    my_step = jnp.sum(jnp.where(group_ids == my_span, step_index, 0))
    step_ids = jnp.arange(gate_table.shape[0], dtype=jnp.int32)
    gate_row = jnp.sum(jnp.where((step_ids == my_step)[:, None], gate_table, 0.0), axis=0)
    return (gate_row[None, :] * shared).astype(jnp.bfloat16)


def solution(mesh):
    in_specs = (
        P(("streams", "span", "seq"), "head"),
        P(("streams", "span", "seq"), "head"),
        P(("streams", "span", "seq"), "head"),
        P("head", "seq"),
        P(None, "head"),
        P("streams"),
        P("streams", None),
    )
    out_specs = P(("streams", "span", "seq"), "head")
    return jax.shard_map(
        on_device, mesh=mesh, in_specs=in_specs, out_specs=out_specs, check_vma=False
    )
```

profile of v0, /device:TPU:28, one launch (start us, length us, event | category | flops | bytes accessed | tf_op | source)
XLA Modules:
  0.0 151.3 jit_solution(9862988004682840681)
XLA Ops:
  6.5 0.0 all-gather.6.cloned.1.call-start
  6.5 0.7 all-gather.6.cloned.1.call-update
  7.3 0.0 all-gather.4.cloned.1.call-start
  7.3 1.9 %copy.16 = bf16[256,640]{0,1:T(8,128)(2,1)} copy(bf16[256,640]{1,0:T(8,128)(2,1)} %param.8) | data formatting | bytes 655360 | tf_op args[1]
  9.2 0.0 all-gather.4.cloned.1.call-update
  9.2 0.0 all-gather.8.cloned.1.call-start
  9.2 0.7 all-gather.8.cloned.1.call-update
  9.9 0.0 reduce-scatter.2.cloned.1.call-start
  10.0 1.1 copy.15
  11.2 0.8 select_reduce_fusion.2
  11.9 0.1 select_reduce_fusion.1
  12.0 29.9 %all-gather.6.cloned.1.call-done = bf16[2048,640]{1,0:T(8,128)(2,1)} async-done(((bf16[256,640]{1,0:T(8,128)(2,1)}), bf16[2048,640]{1,0:T(8,128)(2,1)}) %all-gather.6.cloned.1.call-update) | async-done | bytes 2621456 | tf_op jit(solution)/shard_map/all_gather | solution.py:26
  41.9 3.0 %copy.19 = bf16[2048,640]{0,1:T(8,128)(2,1)S(1)} copy(bf16[2048,640]{1,0:T(8,128)(2,1)} %all-gather.6.cloned.1.call-done) | data formatting | bytes 5242880 | tf_op jit(solution)/shard_map/all_gather | solution.py:26
  44.9 32.1 %all-gather.4.cloned.1.call-done = bf16[2048,640]{0,1:T(8,128)(2,1)} async-done(((bf16[256,640]{0,1:T(8,128)(2,1)}), bf16[2048,640]{0,1:T(8,128)(2,1)}) %all-gather.4.cloned.1.call-update) | async-done | bytes 2621456 | tf_op jit(solution)/shard_map/all_gather | solution.py:25
  77.0 3.7 %fusion = (f32[5,256]{1,0:T(8,128)S(1)}, f32[5,256,2048]{2,1,0:T(8,128)S(1)}) fusion(pred[2048]{0:T(1024)(128)(4,1)S(1)} %broadcast_compare_fusion, bf16[256,5,128]{0,2,1:T(8,128)(2,1)S(1)} %bitcast.18, bf16[2048,5,128]{0,2,1:T(8,128)(2,1)} %bitcast.16), kind=kOutput, calls=%fused_computation.2 | convolution fusion | flops 678951680 | bytes 13442048 | tf_op jit(solution)/shard_map/thd,khd->htk/dot_general | solution.py:34
  80.6 2.6 %fusion.1 = f32[5,256]{1,0:T(8,128)S(1)} fusion(f32[5,256,2048]{2,1,0:T(8,128)S(1)} %get-tuple-element.6, f32[5,256]{1,0:T(8,128)S(1)} %broadcast_maximum_fusion, pred[2048]{0:T(1024)(128)(4,1)S(1)} %broadcast_compare_fusion), kind=kLoop, calls=%fused_computation.3 | loop fusion | flops 13105920 | bytes 10498048 | tf_op jit(solution)/shard_map/reduce_sum | solution.py:45
  83.2 3.3 %fusion.12 = bf16[256,5,128]{0,2,1:T(8,128)(2,1)S(1)} fusion(bf16[2048,5,128]{0,2,1:T(8,128)(2,1)S(1)} %bitcast.17, f32[5,256,2048]{2,1,0:T(8,128)S(1)} %get-tuple-element.6, f32[5,256]{1,0:T(8,128)S(1)} %broadcast_maximum_fusion, pred[2048]{0:T(1024)(128)(4,1)S(1)} %broadcast_compare_fusion, f32[256,5]{0,1:T(8,128)S(1)} %bitcast.20), kind=kOutput, calls=%fused_computation.11 | convolution fusion | flops 684523520 | bytes 13447168 | tf_op jit(solution)/shard_map/htk,khd->htd/dot_general | solution.py:46
  86.5 10.4 %all-gather.8.cloned.1.call-done = bf16[640,5120]{1,0:T(8,128)(2,1)} async-done(((bf16[640,2560]{1,0:T(8,128)(2,1)}), bf16[640,5120]{1,0:T(8,128)(2,1)}) %all-gather.8.cloned.1.call-update) | async-done | bytes 6553616 | tf_op jit(solution)/shard_map/all_gather | solution.py:60
  96.9 0.0 copy-start.1
  96.9 0.0 copy-start
  96.9 6.7 %convolution_convert_fusion = bf16[256,5120]{1,0:T(8,128)(2,1)} fusion(bf16[256,640]{0,1:T(8,128)(2,1)S(1)} %bitcast.19, bf16[640,5120]{1,0:T(8,128)(2,1)} %all-gather.8.cloned.1.call-done), kind=kOutput, calls=%fused_computation.5 | convolution fusion | flops 1679032320 | bytes 9502720 | tf_op jit(solution)/shard_map/dot_general | solution.py:58
  103.5 0.0 reduce-scatter.2.cloned.1.call-update
  103.6 0.0 copy-done.1
  103.6 0.6 select_reduce_fusion.3
  104.2 0.6 iota_compare_fusion.2
  104.9 0.0 copy-done
  104.9 0.1 select_reduce_fusion
  105.0 37.2 %reduce-scatter.2.cloned.1.call-done = bf16[256,2560]{1,0:T(8,128)(2,1)} async-done(((bf16[256,5120]{1,0:T(8,128)(2,1)}), bf16[256,2560]{1,0:T(8,128)(2,1)}) %reduce-scatter.2.cloned.1.call-update) | async-done | bytes 1310736 | tf_op jit(solution)/shard_map/reduce_scatter | solution.py:63
  142.2 2.6 %multiply_convert_fusion = bf16[256,2560]{1,0:T(8,128)(2,1)} fusion(bf16[256,2560]{1,0:T(8,128)(2,1)} %reduce-scatter.2.cloned.1.call-done, f32[2560]{0:T(1024)S(1)} %select_reduce_fusion), kind=kLoop, calls=%fused_computation.8 | loop fusion | flops 1966080 | bytes 2631680 | tf_op jit(solution)/shard_map/convert_element_type | solution.py:69
  (4 shorter events, 0.0 us)
Async XLA Ops:
  6.5 35.4 %all-gather.6.cloned.1.call-start = ((), (), s32[]{:S(2)}) async-start(), calls=%async_computation.2 | async-start | bytes 2949120 | tf_op jit(solution)/shard_map/all_gather | solution.py:26
  7.3 69.7 %all-gather.4.cloned.1.call-start = ((), (), s32[]{:S(2)}) async-start(), calls=%async_computation.1 | async-start | bytes 2949120 | tf_op jit(solution)/shard_map/all_gather | solution.py:25
  9.2 87.7 %all-gather.8.cloned.1.call-start = ((), (), s32[]{:S(2)}) async-start(), calls=%async_computation.3 | async-start | bytes 9830400 | tf_op jit(solution)/shard_map/all_gather | solution.py:60
  9.9 132.3 %reduce-scatter.2.cloned.1.call-start = ((), (), s32[]{:S(2)}) async-start(), calls=%async_computation.4 | async-start | bytes 3932160 | tf_op jit(solution)/shard_map/reduce_scatter | solution.py:63
  96.9 6.7 %copy-start.1 = (s32[4]{0:T(128)S(1)}, s32[4]{0:T(128)}, u32[]{:S(2)}) copy-start(s32[4]{0:T(128)} %param.12) | copy-start | bytes 52
  96.9 8.0 %copy-start = (f32[4,2560]{1,0:T(4,128)S(1)}, f32[4,2560]{1,0:T(4,128)}, u32[]{:S(2)}) copy-start(f32[4,2560]{1,0:T(4,128)} %param.11) | copy-start | bytes 122884
Sparse Core Ops, SparseCore 0:
  9.0 32.8 all-gather.5
  43.5 33.4 all-gather.3
  78.5 18.3 all-gather.7
  103.7 38.4 reduce-scatter.1
where the time goes:
time: 153 us; the launch traced here: 151 us
  waiting for transfers between devices  111 us (73%)
  matrix products  13.6 us (9%)
  between operations  13.2 us (9%)
  other arithmetic  7.42 us (5%)
  local copies, waits for them, and re-layouts  6.01 us (4%)
    reduce_scatter x1, waiting for transfers between devices, on_device(): lax.psum_scatter(projected.astype(jnp.bfloat16), 'head', scatter_dimensio...  37.2 us
    all_gather x1, waiting for transfers between devices, on_device(): key_part = lax.all_gather(key_rows, ('span', 'seq'), axis=0, tiled=True)  32.1 us
    all_gather x1, waiting for transfers between devices, on_device(): value_part = lax.all_gather(value_rows, ('span', 'seq'), axis=0, tiled=True)  29.9 us
    all_gather x1, waiting for transfers between devices, on_device(): lax.all_gather(out_weight, 'seq', axis=1, tiled=True)  10.4 us
    dot_general x1, matrix products, on_device(): jnp.dot(attended, lax.all_gather(out_weight, 'seq', axis=1, tiled=True),...  6.68 us
    dot_general x1, matrix products, on_device(): jnp.einsum('thd,khd->htk', query_three, key_part.reshape(piece_rows, head...  3.67 us
    dot_general x1, matrix products, on_device(): jnp.einsum('htk,khd->htd', probs.astype(jnp.bfloat16), value_part.reshape...  3.29 us
  transfers between devices with their start and end apart: 4, of which 4 were waited for; matrix products, arithmetic and copies ran while one was open for 12% of the time, Pallas kernels for 0%

commit v1 on v0

v1 whole, which is shorter than its diff:
```python
import functools
import math

import jax
import jax.numpy as jnp
from jax import lax
from jax.experimental import pallas as pl
from jax.experimental.pallas import tpu as pltpu
from jax.sharding import PartitionSpec as P

HD = 128
NEG = -1e30
STAT = 16
VMEM_LIMIT = 16 * 1024 * 1024
BRIEF = pl.CostEstimate(flops=1, transcendentals=0, bytes_accessed=1)


def dot(a, b, dims):
    return lax.dot_general(a, b, (dims, ((), ())), preferred_element_type=jnp.float32)


def parts_of(x):
    hi = x.astype(jnp.bfloat16)
    rest = x - hi.astype(jnp.float32)
    mid = rest.astype(jnp.bfloat16)
    low = (rest - mid.astype(jnp.float32)).astype(jnp.bfloat16)
    return hi, mid, low


def write_message(acc, top, out_ref, at):
    rows = acc.shape[0]
    lanes = slice(at, at + HD)
    total = acc[:, HD:]
    live = total > 0.0
    safe = jnp.where(live, total, 1.0)
    out_ref[0:rows, lanes] = (acc[:, :HD] / safe).astype(jnp.bfloat16)
    lse = jnp.where(live, top + jnp.log2(safe), NEG)
    hi, mid, low = parts_of(lse)
    lane = lax.broadcasted_iota(jnp.int32, lse.shape, 1)
    zero = jnp.zeros_like(hi)
    packed = jnp.where(lane == 0, hi, jnp.where(lane == 1, mid, jnp.where(lane == 2, low, zero)))
    row = lax.broadcasted_iota(jnp.int32, (STAT, HD), 0)
    col = lax.broadcasted_iota(jnp.int32, (STAT, HD), 1)
    stats = jnp.zeros((STAT, HD), jnp.float32)
    for block in range(rows // HD):
        pick = jnp.where((row - 3 * block == col) & (col < 3), 1.0, 0.0).astype(jnp.bfloat16)
        stats += dot(pick, packed[block * HD : (block + 1) * HD], ((1,), (1,)))
    out_ref[rows:, lanes] = stats.astype(jnp.bfloat16)


def read_message(msg_ref, rows, at):
    lanes = slice(at, at + HD)
    row = lax.broadcasted_iota(jnp.int32, (STAT, HD), 0)
    blocks = []
    for block in range(rows // HD):
        pick = jnp.where((row >= 3 * block) & (row < 3 * block + 3), 1.0, 0.0).astype(jnp.bfloat16)
        blocks.append(dot(msg_ref[rows:, lanes], pick, ((0,), (0,))))
    return msg_ref[0:rows, lanes].astype(jnp.float32), jnp.concatenate(blocks, axis=0)


def visible_of(role, step, mask_ref):
    span, spans = lax.axis_index("span"), mask_ref.shape[1]
    keys = jnp.maximum(span - step, 0)
    if role == "own":
        there = (span >= step) if step == 0 else (span >= step) & (span != spans - 1)
        return there & (mask_ref[span, keys] == 1)
    return (span == spans - 2) & (span >= step) & (mask_ref[spans - 1, keys] == 1)


def wide(h):
    return slice(2 * h * HD, 2 * (h + 1) * HD)


def attend_kernel(roles, step, span_of_heads, pieces, emit, mask_ref, *refs):
    low, high = span_of_heads
    first = step == 0
    k_ref, v_refs, refs = refs[0], refs[1 : 1 + pieces], refs[1 + pieces :]
    q_refs, refs = refs[: 2 * len(roles)], refs[2 * len(roles) :]
    if not first:
        refs = refs[2 * len(roles) :]
    rows = q_refs[0].shape[0]
    scale = math.log2(math.e) / math.sqrt(HD)

    def values_of(h):
        at = h - low
        for v_ref in v_refs:
            heads = v_ref.shape[1] // HD
            if at < heads:
                return v_ref[:, at * HD : (at + 1) * HD]
            at -= heads

    for i, role in enumerate(roles):
        acc_ref, top_ref = refs[2 * i : 2 * i + 2]
        visible = visible_of(role, step, mask_ref)

        @pl.when(visible)
        def _():
            ones = jnp.ones((k_ref.shape[0], HD), jnp.bfloat16)
            for h in range(low, high):
                lanes = slice(h * HD, (h + 1) * HD)
                k, v = k_ref[:, lanes], jnp.concatenate([values_of(h), ones], axis=1)
                for half in range(2):
                    at = slice(half * rows, (half + 1) * rows)
                    score = dot(q_refs[2 * i + half][:, lanes], k, ((1,), (1,)))
                    peak = jnp.max(score, axis=1, keepdims=True) * scale
                    peak = jnp.broadcast_to(peak, (rows, HD))
                    top = peak if first else jnp.maximum(top_ref[at, lanes], peak)
                    prob = jnp.exp2(score * scale - top[:, :1]).astype(jnp.bfloat16)
                    acc = dot(prob, v, ((1,), (0,)))
                    if not first:
                        fade = jnp.exp2(top_ref[at, lanes] - top)
                        acc += acc_ref[at, wide(h)] * jnp.concatenate([fade, fade], axis=1)
                    acc_ref[at, wide(h)] = acc
                    top_ref[at, lanes] = top

        if first:

            @pl.when(jnp.logical_not(visible))
            def _():
                acc_ref[...] = jnp.zeros(acc_ref.shape, jnp.float32)
                top_ref[...] = jnp.full(top_ref.shape, NEG, jnp.float32)

        if emit:
            def write():
                for h in range(low, high):
                    top = top_ref[rows:, h * HD : (h + 1) * HD]
                    write_message(acc_ref[rows:, wide(h)], top, refs[-1], (h - low) * HD)

            if role == "lent":
                pl.when(lax.axis_index("span") == mask_ref.shape[1] - 2)(write)
            else:
                write()


def attend(mask, roles, step, span_of_heads, key, values, queries, states, emit=False):
    rows, width = key.shape[0], key.shape[1]
    some = span_of_heads[1] - span_of_heads[0]
    state_shape = [
        jax.ShapeDtypeStruct((2 * rows, 2 * width), jnp.float32),
        jax.ShapeDtypeStruct((2 * rows, width), jnp.float32),
    ]
    out_shape = state_shape * len(roles)
    if emit:
        out_shape.append(jax.ShapeDtypeStruct((rows + STAT, some * HD), jnp.bfloat16))
    operands = [key, *values, *queries]
    aliases = {}
    if step:
        aliases = {1 + len(operands) + i: i for i in range(2 * len(roles))}
        for state in states:
            operands += list(state)
    out = pl.pallas_call(
        functools.partial(attend_kernel, roles, step, span_of_heads, len(values), emit),
        out_shape=out_shape,
        in_specs=[pl.BlockSpec(memory_space=pltpu.SMEM)]
        + [pl.BlockSpec(memory_space=pltpu.VMEM)] * len(operands),
        out_specs=[pl.BlockSpec(memory_space=pltpu.VMEM)] * len(out_shape),
        input_output_aliases=aliases,
        compiler_params=pltpu.CompilerParams(vmem_limit_bytes=VMEM_LIMIT),
        cost_estimate=BRIEF,
        name="attend_" + "_".join(roles) + str(step) + str(span_of_heads[0]),
    )(mask, *operands)
    states = [tuple(out[2 * i : 2 * i + 2]) for i in range(len(roles))]
    return (states, out[-1]) if emit else states


def join_kernel(span_of_heads, forward, mask_ref, acc_ref, top_ref, mate_ref, *refs):
    low, high = span_of_heads
    span, spans = lax.axis_index("span"), mask_ref.shape[1]
    out_ref = refs[-1]
    rows = mate_ref.shape[0] - STAT

    def run(messages):
        for h in range(low, high):
            at = (h - low) * HD
            acc, top = acc_ref[0:rows, wide(h)], top_ref[0:rows, h * HD : (h + 1) * HD]
            for ref, is_mate in messages:
                part, lse = read_message(ref, rows, h * HD if is_mate and not forward else at)
                peak = jnp.maximum(top, lse)
                mine, theirs = jnp.exp2(top - peak), jnp.exp2(lse - peak)
                theirs = jnp.where(lse > 0.5 * NEG, theirs, 0.0)
                acc = acc * jnp.concatenate([mine, mine], axis=1) + jnp.concatenate([part * theirs, theirs], axis=1)
                top = peak
            if forward:
                write_message(acc, top, out_ref, at)
            else:
                out_ref[:, at : at + HD] = (acc[:, :HD] / acc[:, HD:]).astype(jnp.bfloat16)

    if forward:
        pl.when(span == spans - 2)(lambda: run([(mate_ref, True)]))
    else:
        pl.when(span == spans - 1)(lambda: run([(mate_ref, True), (refs[0], False)]))
        pl.when(span != spans - 1)(lambda: run([(mate_ref, True)]))


def join(mask, span_of_heads, state, mate, message=None):
    forward = message is None
    rows, width = mate.shape[0] - STAT, (span_of_heads[1] - span_of_heads[0]) * HD
    operands = [*state, mate] + ([] if forward else [message])
    return pl.pallas_call(
        functools.partial(join_kernel, span_of_heads, forward),
        out_shape=jax.ShapeDtypeStruct((rows + STAT if forward else rows, width), jnp.bfloat16),
        in_specs=[pl.BlockSpec(memory_space=pltpu.SMEM)]
        + [pl.BlockSpec(memory_space=pltpu.VMEM)] * len(operands),
        out_specs=pl.BlockSpec(memory_space=pltpu.VMEM),
        compiler_params=pltpu.CompilerParams(vmem_limit_bytes=VMEM_LIMIT),
        cost_estimate=BRIEF,
        name=("forward" if forward else "join") + str(span_of_heads[0]),
    )(mask, *operands)


def project_kernel(groups, tile, step_ref, *refs):
    mine, theirs = refs[:groups], refs[groups : 2 * groups]
    w_own, w_mate, w_far, w_back, gate_ref, out_ref, stage, sems = refs[2 * groups :]
    straight = lax.axis_index("head") == lax.axis_index("seq")
    tiles = out_ref.shape[1] // tile
    gate_row = pl.ds(step_ref[lax.axis_index("span")], 1)

    def copy(t):
        return pltpu.make_async_copy(stage.at[t], out_ref.at[:, t * tile : (t + 1) * tile], sems.at[t])

    def run(w_mine, w_theirs):
        for t in range(tiles):
            lanes = slice(t * tile, (t + 1) * tile)
            total, at = None, 0
            for own_ref, far_ref in zip(mine, theirs):
                width = own_ref.shape[1]
                term = dot(own_ref[...], w_mine[at : at + width, lanes], ((1,), (0,)))
                term += dot(far_ref[...], w_theirs[at : at + width, lanes], ((1,), (0,)))
                total = term if total is None else total + term
                at += width
            stage[t] = (gate_ref[gate_row, lanes] * total).astype(jnp.bfloat16)
            copy(t).start()

    @pl.when(straight)
    def _():
        run(w_own, w_back)

    @pl.when(jnp.logical_not(straight))
    def _():
        run(w_mate, w_far)

    for t in range(tiles):
        copy(t).wait()


def project(step_index, mine, theirs, weights, gate_table):
    rows, columns = mine[0].shape[0], weights[0].shape[1]
    tile = 512
    operands = [*mine, *theirs, *weights, gate_table]
    return pl.pallas_call(
        functools.partial(project_kernel, len(mine), tile),
        out_shape=jax.ShapeDtypeStruct((rows, columns), jnp.bfloat16),
        in_specs=[pl.BlockSpec(memory_space=pltpu.SMEM)]
        + [pl.BlockSpec(memory_space=pltpu.VMEM)] * len(operands),
        out_specs=pl.BlockSpec(memory_space=pl.ANY),
        scratch_shapes=[
            pltpu.VMEM((columns // tile, rows, tile), jnp.bfloat16),
            pltpu.SemaphoreType.DMA((columns // tile,)),
        ],
        compiler_params=pltpu.CompilerParams(vmem_limit_bytes=VMEM_LIMIT),
        cost_estimate=BRIEF,
        name="project",
    )(step_index, *operands)


def after(value, done):
    return lax.optimization_barrier((value, done))[0]


def swap_pairs(count):
    return [(i, count - 1 - i) for i in range(count)]


def on_device(query_rows, key_rows, value_rows, out_weight, gate_table, step_index, block_mask):
    heads = query_rows.shape[1] // HD
    spans, cores, sides = lax.axis_size("span"), lax.axis_size("seq"), lax.axis_size("head")
    split = (heads + 1) // 2
    groups = [(0, split), (split, heads)]
    everyone = (0, heads)
    exchange = sides == cores == 2
    final = spans - 2

    def up(x, step):
        return lax.ppermute(x, "span", [(i, i + 1) for i in range(step - 1, spans - 2)])

    def across(x):
        return lax.ppermute(x, "seq", swap_pairs(cores))

    if exchange:
        pair = ("head", "seq")
        w_far = lax.ppermute(out_weight, pair, [(1, 2), (2, 1)])
    asked = lax.ppermute(query_rows, "span", [(spans - 1, spans - 2)])
    queries = [query_rows, across(query_rows)]
    key, value = key_rows, value_rows
    own = lent = None
    for step in range(final):
        key_next = up(key, step + 1)
        if step + 1 < final:
            value_next = up(value, step + 1)
        else:
            value_next = [up(value[:, a * HD : b * HD], step + 1) for a, b in groups]
        if step == 0:
            (own,) = attend(block_mask, ["own"], 0, everyone, key, [value], queries, [])
            asked = after(asked, own)
            asks = [asked, across(asked)]
            (lent,) = attend(block_mask, ["lent"], 0, everyone, key, [value], asks, [])
            key_next = after(key_next, own)
        else:
            lent, own = attend(
                block_mask, ["lent", "own"], step, everyone, key, [value], asks + queries, [lent, own]
            )
        key = key_next
        value = after(value_next, lent) if step + 1 < final else [after(x, lent) for x in value_next]
    sent, back_up, drafts = [], [(spans - 2, spans - 1)], []
    for g, part in enumerate(groups):
        piece = after(value[g], message) if g else value[g]
        (lent,), draft = attend(block_mask, ["lent"], final, part, key, [piece], asks, [lent], emit=True)
        message = join(block_mask, part, lent, across(draft))
        sent.append(lax.ppermute(message, "span", back_up))
    queries[0] = after(queries[0], message)
    (own,), draft = attend(block_mask, ["own"], final, everyone, key, value, queries, [own], emit=True)
    mate = across(draft)
    mine = [join(block_mask, groups[0], own, mate, sent[0])]
    mine.append(join(block_mask, groups[1], own, mate, after(sent[1], mine[0])))

    if exchange:
        theirs = [lax.ppermute(x, "head", swap_pairs(sides)) for x in mine]
        w_mate = lax.ppermute(after(out_weight, message), pair, [(0, 1), (3, 2)])
        w_back = lax.ppermute(after(w_far, own), pair, [(1, 0), (2, 3)])
        return project(step_index, mine, theirs, [out_weight, w_mate, w_far, w_back], gate_table)
    weight = lax.all_gather(out_weight, "seq", axis=1, tiled=True)
    projected = jnp.dot(jnp.concatenate(mine, axis=1), weight, preferred_element_type=jnp.float32)
    shared = lax.psum_scatter(projected.astype(jnp.bfloat16), "head", scatter_dimension=1, tiled=True)
    gate_row = gate_table[step_index[lax.axis_index("span")]]
    return (gate_row[None, :] * shared.astype(jnp.float32)).astype(jnp.bfloat16)


def solution(mesh):
    in_specs = (
        P(("streams", "span", "seq"), "head"),
        P(("streams", "span", "seq"), "head"),
        P(("streams", "span", "seq"), "head"),
        P("head", "seq"),
        P(None, "head"),
        P("streams"),
        P("streams", None),
    )
    out_specs = P(("streams", "span", "seq"), "head")
    return jax.shard_map(
        on_device, mesh=mesh, in_specs=in_specs, out_specs=out_specs, check_vma=False
    )
```

time: 153 us -> 81.7 us (0.53)
  waiting for transfers between devices: 111 us -> 33.8 us
  starting transfers between devices: 0.12 us -> 31.2 us
  matrix products: 13.6 us -> 0 us
  between operations: 13.2 us -> 0.46 us
  Pallas kernels: 0 us -> 12.2 us
  other arithmetic: 7.42 us -> 0 us
  local copies, waits for them, and re-layouts: 6.01 us -> 3.65 us
    all_gather x3 -> x0, waiting for transfers between devices: 72.3 us -> none  [the longest x1 32.1 us: on_device(): key_part = lax.all_gather(key_rows, ('span', 'seq'), axis=0, tiled=True)]
    reduce_scatter x1 -> x0, waiting for transfers between devices: 37.2 us -> none  [on_device(): lax.psum_scatter(projected.astype(jnp.bfloat16), 'head', scatter_dimensio...]
    ppermute x0 -> x18, waiting for transfers between devices: none -> 33.8 us  [the longest x2 24.4 us: on_device(): sent.append(lax.ppermute(message, 'span', back_up))]
    ppermute x0 -> x18, starting transfers between devices: none -> 31.2 us  [the longest x5 16.8 us: across(): return lax.ppermute(x, 'seq', swap_pairs(cores))]
    dot_general x3 -> x0, matrix products: 13.6 us -> none  [the longest x1 6.68 us: on_device(): jnp.dot(attended, lax.all_gather(out_weight, 'seq', axis=1, tiled=True),...]
    pallas_call x0 -> x11, Pallas kernels: none -> 12.2 us  [the longest x6 5.31 us: attend(): pl.pallas_call(functools.partial(attend_kernel, roles, step, span_of_head...]
    reduce_sum x5 -> x0, other arithmetic: 4.16 us -> none  [the longest x1 2.56 us: on_device(): run_total = jnp.sum(probs, axis=2)]
    all_gather x1 -> x0, local copies, waits for them, and re-layouts: 2.99 us -> none  [on_device(): value_part = lax.all_gather(value_rows, ('span', 'seq'), axis=0, tiled=True)]
  transfers between devices with their start and end apart: 4 -> 18, of which waited for: 4 -> 7; matrix products, arithmetic and copies ran while one was open for 12% -> 0% of each run, Pallas kernels for 0% -> 11%
where the time goes in v1:
time: 81.7 us; the launch traced here: 81.2 us
  waiting for transfers between devices  33.8 us (41%)
  starting transfers between devices  31.2 us (38%)
  Pallas kernels  12.2 us (15%)
  local copies, waits for them, and re-layouts  3.65 us (4%)
    ppermute x2, waiting for transfers between devices, on_device(): sent.append(lax.ppermute(message, 'span', back_up))  24.4 us
    ppermute x5, starting transfers between devices, across(): return lax.ppermute(x, 'seq', swap_pairs(cores))  16.8 us
    ppermute x2, waiting for transfers between devices, on_device(): theirs = [lax.ppermute(x, 'head', swap_pairs(sides)) for x in mine]  5.37 us
    pallas_call x6, Pallas kernels, attend(): pl.pallas_call(functools.partial(attend_kernel, roles, step, span_of_head...  5.31 us
    unnamed x16, local copies, waits for them, and re-layouts  3.61 us
    pallas_call x1, Pallas kernels, project(): pl.pallas_call(functools.partial(project_kernel, len(mine), tile), out_sh...  3.5 us
    ppermute x5, starting transfers between devices, up(): lax.ppermute(x, 'span', [(i, i + 1) for i in range(step - 1, spans - 2)])  3.38 us
    pallas_call x4, Pallas kernels, join(): pl.pallas_call(functools.partial(join_kernel, span_of_heads, forward), ou...  3.34 us
  transfers between devices with their start and end apart: 18, of which 7 were waited for; matrix products, arithmetic and copies ran while one was open for 0% of the time, Pallas kernels for 11%

profile of v1, /device:TPU:28, one launch (start us, length us, event | category | flops | bytes accessed | tf_op | source)
XLA Modules:
  0.0 81.2 jit_solution(13824038817278900786)
XLA Ops:
  0.0 0.9 %collective-permute-start.16 = (bf16[640,2560]{1,0:T(8,128)(2,1)}, bf16[640,2560]{1,0:T(8,128)(2,1)S(1)}, u32[]{:S(2)}, u32[]{:S(2)}) collective-permute-start(bf16[640,2560]{1,0:T(8,128)(2,1)} %refs_4_.3), channel_id=1, source_target_pairs={{1,2},{2,1},{5,6},{6,5},{9,10},{10,9},{13,14},{14,13},{17,18},{18,... | collective-permute-start | bytes 9830408 | tf_op jit(solution)/shard_map/ppermute | solution.py:291
  0.9 2.7 %collective-permute-start.1 = (bf16[256,640]{1,0:T(8,128)(2,1)}, bf16[256,640]{1,0:T(8,128)(2,1)S(1)}, u32[]{:S(2)}, u32[]{:S(2)}) collective-permute-start(bf16[256,640]{1,0:T(8,128)(2,1)} %refs_3_), channel_id=1, source_target_pairs={{0,1},{1,0},{2,3},{3,2},{4,5},{5,4},{6,7},{7,6},{8,9},{9,8},{10,11... | collective-permute-start | bytes 983048 | tf_op jit(solution)/shard_map/ppermute | solution.py:287
  3.6 2.4 %collective-permute-start.4 = (bf16[256,640]{1,0:T(8,128)(2,1)}, bf16[256,640]{1,0:T(8,128)(2,1)S(1)}, u32[]{:S(2)}, u32[]{:S(2)}) collective-permute-start(bf16[256,640]{1,0:T(8,128)(2,1)} %refs_3_), channel_id=1, source_target_pairs={{12,8},{13,9},{14,10},{15,11},{28,24},{29,25},{30,26},{31,27}} | collective-permute-start | bytes 983048 | tf_op jit(solution)/shard_map/ppermute | solution.py:292
  5.9 0.7 collective-permute-start
  6.7 1.0 %copy-done.1 = bf16[256,640]{1,0:T(8,128)(2,1)S(1)} copy-done((bf16[256,640]{1,0:T(8,128)(2,1)S(1)}, bf16[256,640]{1,0:T(8,128)(2,1)}, u32[]{:S(2)}) %copy-start.1) | copy-done | bytes 327704
  7.6 1.0 %copy-done.3 = bf16[256,640]{1,0:T(8,128)(2,1)S(1)} copy-done((bf16[256,640]{1,0:T(8,128)(2,1)S(1)}, bf16[256,640]{1,0:T(8,128)(2,1)}, u32[]{:S(2)}) %copy-start.3) | copy-done | bytes 327704
  8.6 1.0 %copy-done.4 = bf16[256,640]{1,0:T(8,128)(2,1)S(1)} copy-done((bf16[256,640]{1,0:T(8,128)(2,1)S(1)}, bf16[256,640]{1,0:T(8,128)(2,1)}, u32[]{:S(2)}) %copy-start.4) | copy-done | bytes 327704
  9.6 0.7 copy-done.5
  10.3 1.6 %attend_own00.1 = (f32[512,1280]{1,0:T(8,128)S(1)}, f32[512,640]{1,0:T(8,128)S(1)}) custom-call(s32[4,4]{1,0:T(4,128)S(1)} %copy-done.5, bf16[256,640]{1,0:T(8,128)(2,1)S(1)} %copy-done.3, bf16[256,640]{1,0:T(8,128)(2,1)S(1)} %copy-done.4, bf16[256,640]{1,0:T(8,128)(2,1)S(1)} %copy-done.1, bf16[256,640]{1,0:T(8,128)(2,1)S(1)} %collective-permute-done.1.refs_3_.refs_5_.refs_4_), custom_call_target="tpu_custom_call" | custom-call | flops 1 | bytes 1 | tf_op jit(solution)/shard_map/attend_own00/pallas_call | solution.py:151
  11.9 1.5 %collective-permute-done.4.refs_2_ = bf16[256,640]{1,0:T(8,128)(2,1)S(1)} collective-permute-done((bf16[256,640]{1,0:T(8,128)(2,1)}, bf16[256,640]{1,0:T(8,128)(2,1)S(1)}, u32[]{:S(2)}, u32[]{:S(2)}) %collective-permute-start.4) | collective-permute-done | bytes 327712 | tf_op jit(solution)/shard_map/ppermute | solution.py:292
  13.4 0.7 collective-permute-start.3
  14.1 0.7 collective-permute-start.2
  15.0 0.8 %attend_lent00.1 = (f32[512,1280]{1,0:T(8,128)S(1)}, f32[512,640]{1,0:T(8,128)S(1)}) custom-call(s32[4,4]{1,0:T(4,128)S(1)} %copy-done.5, bf16[256,640]{1,0:T(8,128)(2,1)S(1)} %copy-done.3, bf16[256,640]{1,0:T(8,128)(2,1)S(1)} %copy-done.4, bf16[256,640]{1,0:T(8,128)(2,1)S(1)} %collective-permute-done.4.refs_2_, ...), custom_call_target="tpu_custom_call" | custom-call | flops 1 | bytes 1 | tf_op jit(solution)/shard_map/attend_lent00/pallas_call | solution.py:151
  15.9 0.7 collective-permute-start.6
  16.6 0.7 collective-permute-start.7
  17.3 0.6 attend_lent_own10.1
  17.9 0.6 attend_lent20.1
  18.9 1.2 %collective-permute-done.8.mate_ref = bf16[272,384]{1,0:T(8,128)(2,1)S(1)} collective-permute-done((bf16[272,384]{1,0:T(8,128)(2,1)S(1)}, bf16[272,384]{1,0:T(8,128)(2,1)S(1)}, u32[]{:S(2)}, u32[]{:S(2)}) %collective-permute-start.8) | collective-permute-done | bytes 208928 | tf_op jit(solution)/shard_map/ppermute | solution.py:287
  21.6 1.1 %collective-permute-done.9.mate_ref = bf16[272,256]{1,0:T(8,128)(2,1)S(1)} collective-permute-done((bf16[272,256]{1,0:T(8,128)(2,1)S(1)}, bf16[272,256]{1,0:T(8,128)(2,1)S(1)}, u32[]{:S(2)}, u32[]{:S(2)}) %collective-permute-start.9) | collective-permute-done | bytes 139296 | tf_op jit(solution)/shard_map/ppermute | solution.py:287
  23.3 2.6 %collective-permute-start.15 = (bf16[640,2560]{1,0:T(8,128)(2,1)S(1)}, bf16[640,2560]{1,0:T(8,128)(2,1)S(1)}, u32[]{:S(2)}, u32[]{:S(2)}) collective-permute-start(bf16[640,2560]{1,0:T(8,128)(2,1)S(1)} %copy-done), channel_id=1, source_target_pairs={{0,1},{3,2},{4,5},{7,6},{8,9},{11,10},{12,13},{15,14},{16,17},{19,... | collective-permute-start | bytes 9830408 | tf_op jit(solution)/shard_map/ppermute | solution.py:328
  25.9 1.1 %attend_own20.1 = (f32[512,1280]{1,0:T(8,128)S(1)}, f32[512,640]{1,0:T(8,128)S(1)}, bf16[272,640]{1,0:T(8,128)(2,1)S(1)}) custom-call(s32[4,4]{1,0:T(4,128)S(1)} %copy-done.5, bf16[256,640]{1,0:T(8,128)(2,1)S(1)} %collective-permute-done.2.refs_0_, ...), custom_call_target="tpu_custom_call", output_to_operand_aliasing={{0}: (6, {}), {1}: (7, {})} | custom-call | flops 1 | bytes 1 | tf_op jit(solution)/shard_map/attend_own20/pallas_call | solution.py:151
  26.9 1.3 %collective-permute-start.17 = (bf16[640,2560]{1,0:T(8,128)(2,1)S(1)}, bf16[640,2560]{1,0:T(8,128)(2,1)S(1)}, u32[]{:S(2)}, u32[]{:S(2)}) collective-permute-start(bf16[640,2560]{1,0:T(8,128)(2,1)S(1)} %collective-permute-done.16.refs_6_), channel_id=1, source_target_pairs={{1,0},{2,3},{5,4},{6,7},{9,8},{10,11},{13,12},{14,15},{17,16},{18,... | collective-permute-start | bytes 9830408 | tf_op jit(solution)/shard_map/ppermute | solution.py:329
  28.2 13.4 %collective-permute-start.10 = (bf16[272,640]{1,0:T(8,128)(2,1)S(1)}, bf16[272,640]{1,0:T(8,128)(2,1)S(1)}, u32[]{:S(2)}, u32[]{:S(2)}) collective-permute-start(bf16[272,640]{1,0:T(8,128)(2,1)S(1)} %get-tuple-element.55), channel_id=1, source_target_pairs={{0,1},{1,0},{2,3},{3,2},{4,5},{5,4},{6,7},{7,6},{8,9},{9,8},{10,11... | collective-permute-start | bytes 1044488 | tf_op jit(solution)/shard_map/ppermute | solution.py:287
  41.6 1.3 %collective-permute-start.11 = (bf16[272,384]{1,0:T(8,128)(2,1)S(1)}, bf16[272,384]{1,0:T(8,128)(2,1)S(1)}, u32[]{:S(2)}, u32[]{:S(2)}) collective-permute-start(bf16[272,384]{1,0:T(8,128)(2,1)S(1)} %forward0.1), channel_id=1, source_target_pairs={{8,12},{9,13},{10,14},{11,15},{24,28},{25,29},{26,30},{27,31}} | collective-permute-start | bytes 626696 | tf_op jit(solution)/shard_map/ppermute | solution.py:319
  42.9 1.3 %collective-permute-start.12 = (bf16[272,256]{1,0:T(8,128)(2,1)S(1)}, bf16[272,256]{1,0:T(8,128)(2,1)S(1)}, u32[]{:S(2)}, u32[]{:S(2)}) collective-permute-start(bf16[272,256]{1,0:T(8,128)(2,1)S(1)} %forward3.1), channel_id=1, source_target_pairs={{8,12},{9,13},{10,14},{11,15},{24,28},{25,29},{26,30},{27,31}} | collective-permute-start | bytes 417800 | tf_op jit(solution)/shard_map/ppermute | solution.py:319
  44.2 23.6 %collective-permute-done.11.refs_0_ = bf16[272,384]{1,0:T(8,128)(2,1)S(1)} collective-permute-done((bf16[272,384]{1,0:T(8,128)(2,1)S(1)}, bf16[272,384]{1,0:T(8,128)(2,1)S(1)}, u32[]{:S(2)}, u32[]{:S(2)}) %collective-permute-start.11) | collective-permute-done | bytes 208928 | tf_op jit(solution)/shard_map/ppermute | solution.py:319
  67.8 1.2 %join0.1.refs_0_ = bf16[256,384]{1,0:T(8,128)(2,1)S(1)} custom-call(s32[4,4]{1,0:T(4,128)S(1)} %copy-done.5, f32[512,1280]{1,0:T(8,128)S(1)} %get-tuple-element.53.acc_ref, f32[512,640]{1,0:T(8,128)S(1)} %get-tuple-element.54.top_ref, bf16[272,640]{1,0:T(8,128)(2,1)S(1)} %collective-permute-done.10.mate_ref, bf16[272,384]{1,0:T(8,128)(2,1)S(1)} %collective-permute-done.11.refs_0_), custom_call_target="tpu_custom_call" | custom-call | flops 1 | bytes 1 | tf_op jit(solution)/shard_map/join0/pallas_call | solution.py:199
  69.4 0.8 collective-permute-done.12.refs_0_
  70.2 1.0 %join3.1.refs_1_ = bf16[256,256]{1,0:T(8,128)(2,1)S(1)} custom-call(s32[4,4]{1,0:T(4,128)S(1)} %copy-done.5, f32[512,1280]{1,0:T(8,128)S(1)} %get-tuple-element.53.acc_ref, f32[512,640]{1,0:T(8,128)S(1)} %get-tuple-element.54.top_ref, bf16[272,640]{1,0:T(8,128)(2,1)S(1)} %collective-permute-done.10.mate_ref, bf16[272,256]{1,0:T(8,128)(2,1)S(1)} %collective-permute-done.12.refs_0_), custom_call_target="tpu_custom_call" | custom-call | flops 1 | bytes 1 | tf_op jit(solution)/shard_map/join3/pallas_call | solution.py:199
  71.2 1.0 %collective-permute-start.14 = (bf16[256,256]{1,0:T(8,128)(2,1)S(1)}, bf16[256,256]{1,0:T(8,128)(2,1)S(1)}, u32[]{:S(2)}, u32[]{:S(2)}) collective-permute-start(bf16[256,256]{1,0:T(8,128)(2,1)S(1)} %join3.1.refs_1_), channel_id=1, source_target_pairs={{0,2},{2,0},{1,3},{3,1},{4,6},{6,4},{5,7},{7,5},{8,10},{10,8},{9,1... | collective-permute-start | bytes 393224 | tf_op jit(solution)/shard_map/ppermute | solution.py:327
  72.2 5.4 %collective-permute-done.14.refs_3_ = bf16[256,256]{1,0:T(8,128)(2,1)S(1)} collective-permute-done((bf16[256,256]{1,0:T(8,128)(2,1)S(1)}, bf16[256,256]{1,0:T(8,128)(2,1)S(1)}, u32[]{:S(2)}, u32[]{:S(2)}) %collective-permute-start.14) | collective-permute-done | bytes 131104 | tf_op jit(solution)/shard_map/ppermute | solution.py:327
  77.6 3.5 %project.1 = bf16[256,2560]{1,0:T(8,128)(2,1)} custom-call(s32[4]{0:T(128)S(1)} %copy-done.7, bf16[256,384]{1,0:T(8,128)(2,1)S(1)} %join0.1.refs_0_, bf16[256,256]{1,0:T(8,128)(2,1)S(1)} %join3.1.refs_1_, bf16[256,384]{1,0:T(8,128)(2,1)S(1)} %collective-permute-done.13.refs_2_, bf16[256,256]{1,0:T(8,128)(2,1)S(1)} %collective-permute-done.14.refs_3_, ...), custom_call_target="tpu_custom_call" | custom-call | flops 1 | bytes 1 | tf_op jit(solution)/shard_map/project/pallas_call | solution.py:250
  (33 shorter events, 3.1 us)
Async XLA Ops:
  0.0 26.9 %collective-permute-start.16 = (bf16[640,2560]{1,0:T(8,128)(2,1)}, bf16[640,2560]{1,0:T(8,128)(2,1)S(1)}, u32[]{:S(2)}, u32[]{:S(2)}) collective-permute-start(bf16[640,2560]{1,0:T(8,128)(2,1)} %refs_4_.3), channel_id=1, source_target_pairs={{1,2},{2,1},{5,6},{6,5},{9,10},{10,9},{13,14},{14,13},{17,18},{18,... | collective-permute-start | bytes 9830408 | tf_op jit(solution)/shard_map/ppermute | solution.py:291
  0.9 5.8 %collective-permute-start.1 = (bf16[256,640]{1,0:T(8,128)(2,1)}, bf16[256,640]{1,0:T(8,128)(2,1)S(1)}, u32[]{:S(2)}, u32[]{:S(2)}) collective-permute-start(bf16[256,640]{1,0:T(8,128)(2,1)} %refs_3_), channel_id=1, source_target_pairs={{0,1},{1,0},{2,3},{3,2},{4,5},{5,4},{6,7},{7,6},{8,9},{9,8},{10,11... | collective-permute-start | bytes 983048 | tf_op jit(solution)/shard_map/ppermute | solution.py:287
  3.6 9.8 %collective-permute-start.4 = (bf16[256,640]{1,0:T(8,128)(2,1)}, bf16[256,640]{1,0:T(8,128)(2,1)S(1)}, u32[]{:S(2)}, u32[]{:S(2)}) collective-permute-start(bf16[256,640]{1,0:T(8,128)(2,1)} %refs_3_), channel_id=1, source_target_pairs={{12,8},{13,9},{14,10},{15,11},{28,24},{29,25},{30,26},{31,27}} | collective-permute-start | bytes 983048 | tf_op jit(solution)/shard_map/ppermute | solution.py:292
  5.9 8.1 %collective-permute-start = (bf16[256,640]{1,0:T(8,128)(2,1)}, bf16[256,640]{1,0:T(8,128)(2,1)S(1)}, u32[]{:S(2)}, u32[]{:S(2)}) collective-permute-start(bf16[256,640]{1,0:T(8,128)(2,1)} %refs_0_.3), channel_id=1, source_target_pairs={{0,4},{4,8},{1,5},{5,9},{2,6},{6,10},{3,7},{7,11},{16,20},{20,24},... | collective-permute-start | bytes 983048 | tf_op jit(solution)/shard_map/ppermute | solution.py:284
  6.6 1.0 %copy-start.1 = (bf16[256,640]{1,0:T(8,128)(2,1)S(1)}, bf16[256,640]{1,0:T(8,128)(2,1)}, u32[]{:S(2)}) copy-start(bf16[256,640]{1,0:T(8,128)(2,1)} %refs_3_) | copy-start | bytes 983044
  7.6 1.0 %copy-start.3 = (bf16[256,640]{1,0:T(8,128)(2,1)S(1)}, bf16[256,640]{1,0:T(8,128)(2,1)}, u32[]{:S(2)}) copy-start(bf16[256,640]{1,0:T(8,128)(2,1)} %refs_0_.3) | copy-start | bytes 983044
  8.6 1.0 %copy-start.4 = (bf16[256,640]{1,0:T(8,128)(2,1)S(1)}, bf16[256,640]{1,0:T(8,128)(2,1)}, u32[]{:S(2)}) copy-start(bf16[256,640]{1,0:T(8,128)(2,1)} %refs_1_.3) | copy-start | bytes 983044
  9.6 0.7 copy-start.5
  10.3 7.0 %copy-start.2 = (bf16[256,640]{1,0:T(8,128)(2,1)S(1)}, bf16[256,640]{1,0:T(8,128)(2,1)}, u32[]{:S(2)}) copy-start(bf16[256,640]{1,0:T(8,128)(2,1)} %refs_3_) | copy-start | bytes 983044
  13.4 1.6 %collective-permute-start.5 = (bf16[256,640]{1,0:T(8,128)(2,1)S(1)}, bf16[256,640]{1,0:T(8,128)(2,1)S(1)}, u32[]{:S(2)}, u32[]{:S(2)}) collective-permute-start(bf16[256,640]{1,0:T(8,128)(2,1)S(1)} %collective-permute-done.4.refs_2_), channel_id=1, source_target_pairs={{0,1},{1,0},{2,3},{3,2},{4,5},{5,4},{6,7},{7,6},{8,9},{9,8},{10,11... | collective-permute-start | bytes 983048 | tf_op jit(solution)/shard_map/ppermute | solution.py:287
  13.4 2.5 %collective-permute-start.3 = (bf16[256,640]{1,0:T(8,128)(2,1)S(1)}, bf16[256,640]{1,0:T(8,128)(2,1)S(1)}, u32[]{:S(2)}, u32[]{:S(2)}) collective-permute-start(bf16[256,640]{1,0:T(8,128)(2,1)S(1)} %copy-done.4), channel_id=1, source_target_pairs={{0,4},{4,8},{1,5},{5,9},{2,6},{6,10},{3,7},{7,11},{16,20},{20,24},... | collective-permute-start | bytes 983048 | tf_op jit(solution)/shard_map/ppermute | solution.py:284
  14.1 3.8 %collective-permute-start.2 = (bf16[256,640]{1,0:T(8,128)(2,1)S(1)}, bf16[256,640]{1,0:T(8,128)(2,1)S(1)}, u32[]{:S(2)}, u32[]{:S(2)}) collective-permute-start(bf16[256,640]{1,0:T(8,128)(2,1)S(1)} %collective-permute-done.refs_0_), channel_id=1, source_target_pairs={{4,8},{5,9},{6,10},{7,11},{20,24},{21,25},{22,26},{23,27}} | collective-permute-start | bytes 983048 | tf_op jit(solution)/shard_map/ppermute | solution.py:284
  15.9 2.0 %collective-permute-start.6 = (bf16[256,384]{1,0:T(8,128)(2,1)S(1)}, bf16[256,384]{1,0:T(8,128)(2,1)S(1)}, u32[]{:S(2)}, u32[]{:S(2)}) collective-permute-start(bf16[256,384]{1,0:T(8,128)(2,1)S(1)} %slice.6), channel_id=1, source_target_pairs={{4,8},{5,9},{6,10},{7,11},{20,24},{21,25},{22,26},{23,27}} | collective-permute-start | bytes 589832 | tf_op jit(solution)/shard_map/ppermute | solution.py:284
  16.6 1.3 %collective-permute-start.7 = (bf16[256,256]{1,0:T(8,128)(2,1)S(1)}, bf16[256,256]{1,0:T(8,128)(2,1)S(1)}, u32[]{:S(2)}, u32[]{:S(2)}) collective-permute-start(bf16[256,256]{1,0:T(8,128)(2,1)S(1)} %slice.7), channel_id=1, source_target_pairs={{4,8},{5,9},{6,10},{7,11},{20,24},{21,25},{22,26},{23,27}} | collective-permute-start | bytes 393224 | tf_op jit(solution)/shard_map/ppermute | solution.py:284
  18.5 1.5 %collective-permute-start.8 = (bf16[272,384]{1,0:T(8,128)(2,1)S(1)}, bf16[272,384]{1,0:T(8,128)(2,1)S(1)}, u32[]{:S(2)}, u32[]{:S(2)}) collective-permute-start(bf16[272,384]{1,0:T(8,128)(2,1)S(1)} %get-tuple-element.45), channel_id=1, source_target_pairs={{0,1},{1,0},{2,3},{3,2},{4,5},{5,4},{6,7},{7,6},{8,9},{9,8},{10,11... | collective-permute-start | bytes 626696 | tf_op jit(solution)/shard_map/ppermute | solution.py:287
  21.3 2.0 %copy-start = (bf16[640,2560]{1,0:T(8,128)(2,1)S(1)}, bf16[640,2560]{1,0:T(8,128)(2,1)}, u32[]{:S(2)}) copy-start(bf16[640,2560]{1,0:T(8,128)(2,1)} %refs_4_.3) | copy-start | bytes 9830404
  21.3 1.4 %collective-permute-start.9 = (bf16[272,256]{1,0:T(8,128)(2,1)S(1)}, bf16[272,256]{1,0:T(8,128)(2,1)S(1)}, u32[]{:S(2)}, u32[]{:S(2)}) collective-permute-start(bf16[272,256]{1,0:T(8,128)(2,1)S(1)} %get-tuple-element.49), channel_id=1, source_target_pairs={{0,1},{1,0},{2,3},{3,2},{4,5},{5,4},{6,7},{7,6},{8,9},{9,8},{10,11... | collective-permute-start | bytes 417800 | tf_op jit(solution)/shard_map/ppermute | solution.py:287
  23.3 54.3 %collective-permute-start.15 = (bf16[640,2560]{1,0:T(8,128)(2,1)S(1)}, bf16[640,2560]{1,0:T(8,128)(2,1)S(1)}, u32[]{:S(2)}, u32[]{:S(2)}) collective-permute-start(bf16[640,2560]{1,0:T(8,128)(2,1)S(1)} %copy-done), channel_id=1, source_target_pairs={{0,1},{3,2},{4,5},{7,6},{8,9},{11,10},{12,13},{15,14},{16,17},{19,... | collective-permute-start | bytes 9830408 | tf_op jit(solution)/shard_map/ppermute | solution.py:328
  26.9 50.6 %collective-permute-start.17 = (bf16[640,2560]{1,0:T(8,128)(2,1)S(1)}, bf16[640,2560]{1,0:T(8,128)(2,1)S(1)}, u32[]{:S(2)}, u32[]{:S(2)}) collective-permute-start(bf16[640,2560]{1,0:T(8,128)(2,1)S(1)} %collective-permute-done.16.refs_6_), channel_id=1, source_target_pairs={{1,0},{2,3},{5,4},{6,7},{9,8},{10,11},{13,12},{14,15},{17,16},{18,... | collective-permute-start | bytes 9830408 | tf_op jit(solution)/shard_map/ppermute | solution.py:329
  28.2 39.6 %collective-permute-start.10 = (bf16[272,640]{1,0:T(8,128)(2,1)S(1)}, bf16[272,640]{1,0:T(8,128)(2,1)S(1)}, u32[]{:S(2)}, u32[]{:S(2)}) collective-permute-start(bf16[272,640]{1,0:T(8,128)(2,1)S(1)} %get-tuple-element.55), channel_id=1, source_target_pairs={{0,1},{1,0},{2,3},{3,2},{4,5},{5,4},{6,7},{7,6},{8,9},{9,8},{10,11... | collective-permute-start | bytes 1044488 | tf_op jit(solution)/shard_map/ppermute | solution.py:287
  41.6 26.2 %collective-permute-start.11 = (bf16[272,384]{1,0:T(8,128)(2,1)S(1)}, bf16[272,384]{1,0:T(8,128)(2,1)S(1)}, u32[]{:S(2)}, u32[]{:S(2)}) collective-permute-start(bf16[272,384]{1,0:T(8,128)(2,1)S(1)} %forward0.1), channel_id=1, source_target_pairs={{8,12},{9,13},{10,14},{11,15},{24,28},{25,29},{26,30},{27,31}} | collective-permute-start | bytes 626696 | tf_op jit(solution)/shard_map/ppermute | solution.py:319
  42.9 27.3 %collective-permute-start.12 = (bf16[272,256]{1,0:T(8,128)(2,1)S(1)}, bf16[272,256]{1,0:T(8,128)(2,1)S(1)}, u32[]{:S(2)}, u32[]{:S(2)}) collective-permute-start(bf16[272,256]{1,0:T(8,128)(2,1)S(1)} %forward3.1), channel_id=1, source_target_pairs={{8,12},{9,13},{10,14},{11,15},{24,28},{25,29},{26,30},{27,31}} | collective-permute-start | bytes 417800 | tf_op jit(solution)/shard_map/ppermute | solution.py:319
  69.0 8.6 %copy-start.6 = (f32[4,2560]{1,0:T(4,128)S(1)}, f32[4,2560]{1,0:T(4,128)}, u32[]{:S(2)}) copy-start(f32[4,2560]{1,0:T(4,128)} %refs_8_.1) | copy-start | bytes 122884
  69.0 8.6 %copy-start.7 = (s32[4]{0:T(128)S(1)}, s32[4]{0:T(128)}, u32[]{:S(2)}) copy-start(s32[4]{0:T(128)} %step_ref.1) | copy-start | bytes 52
  69.0 8.6 %collective-permute-start.13 = (bf16[256,384]{1,0:T(8,128)(2,1)S(1)}, bf16[256,384]{1,0:T(8,128)(2,1)S(1)}, u32[]{:S(2)}, u32[]{:S(2)}) collective-permute-start(bf16[256,384]{1,0:T(8,128)(2,1)S(1)} %join0.1.refs_0_), channel_id=1, source_target_pairs={{0,2},{2,0},{1,3},{3,1},{4,6},{6,4},{5,7},{7,5},{8,10},{10,8},{9,1... | collective-permute-start | bytes 589832 | tf_op jit(solution)/shard_map/ppermute | solution.py:327
  71.2 6.3 %collective-permute-start.14 = (bf16[256,256]{1,0:T(8,128)(2,1)S(1)}, bf16[256,256]{1,0:T(8,128)(2,1)S(1)}, u32[]{:S(2)}, u32[]{:S(2)}) collective-permute-start(bf16[256,256]{1,0:T(8,128)(2,1)S(1)} %join3.1.refs_1_), channel_id=1, source_target_pairs={{0,2},{2,0},{1,3},{3,1},{4,6},{6,4},{5,7},{7,5},{8,10},{10,8},{9,1... | collective-permute-start | bytes 393224 | tf_op jit(solution)/shard_map/ppermute | solution.py:327
